TPU v7x, 32 devices: a whole 2x2x4 slice. The times are simulated.
32 devices in a mesh: row: 8 (over z, x), col: 4 (over y, core).
Axes of the slice: x: 2, y: 2, z: 4, core: 2. Of those that a mesh axis runs over, the one named last changes fastest.
Arguments:
- affinity: bfloat16 [32768, 8192], P('row', 'col'), may hold values from -250 to 250
- seed_values: int32 [16], replicated, may hold values from 0 to 1073741823
- sku_ids: int32 [8192], P('col'), may hold values from 0 to 8191, each once
Outputs:
- range_basis: float32 [16, 32768], P(None, ('row', 'col'))
- range_factor: float32 [16, 16], replicated
All inputs are finite; a program needn't handle non-finite values.
Results may differ from a plain program's by a relative error of at most 0.0046.
Values may be sent and summed in bfloat16 or wider, within the bound.
A program may use at most 64 MiB of HBM per device.

v0:
```python
import math
import jax
import jax.numpy as jnp
from jax import lax
from jax.sharding import PartitionSpec as P

ITERS = 2
mix_first = -2048144789
mix_second = -1028477387
golden = -1640531535
salt_value = 1540483477


def shifted(value, amount):
    return lax.shift_right_logical(value, jnp.full(value.shape, amount, jnp.int32))


def scramble(value):
    value = jnp.bitwise_xor(value, shifted(value, 16))
    value = value * jnp.int32(mix_first)
    value = jnp.bitwise_xor(value, shifted(value, 13))
    value = value * jnp.int32(mix_second)
    return jnp.bitwise_xor(value, shifted(value, 16))


def test_matrix(seed_values, sku_ids, total_columns):
    first = scramble(jnp.bitwise_xor(seed_values[:, None], sku_ids[None, :] * jnp.int32(golden)))
    second = scramble(jnp.bitwise_xor(first, jnp.int32(salt_value)))
    uniform_a = (shifted(first, 9) + 1).astype(jnp.float32) / 8388608.0
    uniform_b = (shifted(second, 9) + 1).astype(jnp.float32) / 8388608.0
    gauss = jnp.sqrt(-2.0 * jnp.log(uniform_a)) * jnp.cos(6.283185307179586 * uniform_b)
    return (gauss / math.sqrt(total_columns)).astype(jnp.bfloat16)


def lower_solve(lower, right):
    return lax.linalg.triangular_solve(lower, right, left_side=True, lower=True)


def body(affinity, seed_values, sku_ids):
    col_count = lax.axis_size("col")
    total_columns = sku_ids.shape[0] * col_count
    local_rows = affinity.shape[0]
    piece_rows = local_rows // col_count
    total_rows = local_rows * lax.axis_size("row")
    inv_root = 1.0 / math.sqrt(total_columns)

    def project(left):
        return lax.dot_general(
            left, affinity, (((1,), (1,)), ((), ())), preferred_element_type=jnp.float32
        )

    omega = test_matrix(seed_values, sku_ids, total_columns)
    partial_sketch = project(omega)
    for repeat in range(ITERS + 1):
        sketch = lax.psum(partial_sketch, "col")
        gram = lax.psum(
            jnp.dot(
                sketch,
                sketch.T,
                precision=lax.Precision.HIGHEST,
                preferred_element_type=jnp.float32,
            ),
            "row",
        )
        lower = jnp.linalg.cholesky(gram)
        ortho = lower_solve(lower, sketch)
        if repeat < ITERS:
            back_part = jnp.dot(
                ortho.astype(jnp.bfloat16), affinity, preferred_element_type=jnp.float32
            )
        else:
            start_row = lax.axis_index("col") * piece_rows
            ortho = lax.dynamic_slice_in_dim(ortho, start_row, piece_rows, 1)
        if repeat < ITERS:
            back = lax.psum(back_part, "row")
            partial_sketch = project(back.astype(jnp.bfloat16)) * inv_root
    scale = math.sqrt(total_rows)
    return (ortho * scale, lower.T / scale)


def solution(mesh):
    placed = (P("row", "col"), P(), P("col"))
    return jax.shard_map(
        body, mesh=mesh, in_specs=placed, out_specs=(P(None, ("row", "col")), P()), check_vma=False
    )
```

profile of v0, /device:TPU:0, one launch (start us, length us, event | category | flops | bytes accessed | tf_op | source)
XLA Modules:
  0.0 315.6 jit_solution(10747152659197352157)
XLA Ops:
  7.2 0.0 all-reduce.6.cloned.1.call-start
  7.2 0.7 broadcast_multiply_fusion
  7.9 11.5 %fusion.12 = f32[16,4096]{1,0:T(8,128)} fusion(bf16[4096,2048]{1,0:T(8,128)(2,1)} %param.6, s32[2048]{0:T(1024)S(1)} %broadcast_multiply_fusion, s32[16]{0:T(128)} %param.7), kind=kOutput, calls=%fused_computation.22 | convolution fusion | flops 269418496 | bytes 17047616 | tf_op jit(solution)/shard_map/dot_general | solution.py:48
  19.5 0.0 all-reduce.6.cloned.1.call-update
  19.5 0.0 all-reduce.8.cloned.1.call-start
  19.5 35.1 %all-reduce.6.cloned.1.call-done = f32[16,4096]{1,0:T(8,128)} async-done(((f32[16,4096]{1,0:T(8,128)}), f32[16,4096]{1,0:T(8,128)}) %all-reduce.6.cloned.1.call-update) | async-done | bytes 262160 | tf_op jit(solution)/shard_map/psum | solution.py:55
  54.6 1.5 fusion.54
  56.1 21.6 %psum.57 = f32[16,16]{0,1:T(8,128)S(1)} all-reduce(f32[16,16]{0,1:T(8,128)S(1)} %fusion.54), channel_id=1, replica_groups=mesh['row'=8,'col'=4] {'row'}, use_global_device_ids=true, to_apply=%region_1.0 | all-reduce | flops 256 | bytes 2048 | tf_op jit(solution)/shard_map/psum | solution.py:56
  77.7 0.1 copy.6
  77.8 1.5 cholesky.59
  79.3 0.6 compare_reduce_fusion.2
  79.9 0.6 fusion.29
  80.6 1.2 custom-call.7
  81.8 1.4 convolution_convert_fusion.1
  83.2 8.0 %fusion.55 = f32[16,2048]{1,0:T(8,128)S(1)} fusion(bf16[16,4096]{1,0:T(8,128)(2,1)S(1)} %convolution_convert_fusion.1, bf16[4096,2048]{1,0:T(8,128)(2,1)} %param.6), kind=kOutput, calls=%fused_computation.79 | convolution fusion | flops 268435456 | bytes 17039360 | tf_op jit(solution)/shard_map/dot_general | solution.py:68
  91.3 34.2 %all-reduce.11 = bf16[16,2048]{1,0:T(8,128)(2,1)S(1)} all-reduce(f32[16,2048]{1,0:T(8,128)S(1)} %fusion.55), channel_id=1, replica_groups=mesh['row'=8,'col'=4] {'row'}, use_global_device_ids=true, to_apply=%region_4.7 | all-reduce | flops 32768 | bytes 196608 | tf_op jit(solution)/shard_map/psum | solution.py:75
  125.5 10.9 %convolution_multiply_fusion.1 = f32[16,4096]{1,0:T(8,128)} fusion(bf16[4096,2048]{1,0:T(8,128)(2,1)} %param.6, bf16[16,2048]{1,0:T(8,128)(2,1)S(1)} %all-reduce.11), kind=kOutput, calls=%fused_computation.1 | convolution fusion | flops 268500992 | bytes 17104896 | tf_op jit(solution)/shard_map/dot_general | solution.py:48
  136.4 0.0 all-reduce.8.cloned.1.call-update
  136.4 0.0 all-reduce.10.cloned.1.call-start
  136.5 30.3 %all-reduce.8.cloned.1.call-done = f32[16,4096]{1,0:T(8,128)} async-done(((f32[16,4096]{1,0:T(8,128)}), f32[16,4096]{1,0:T(8,128)}) %all-reduce.8.cloned.1.call-update) | async-done | bytes 262160 | tf_op jit(solution)/shard_map/psum | solution.py:55
  166.8 1.5 fusion.56
  168.3 21.8 %psum.60 = f32[16,16]{0,1:T(8,128)S(1)} all-reduce(f32[16,16]{0,1:T(8,128)S(1)} %fusion.56), channel_id=1, replica_groups=mesh['row'=8,'col'=4] {'row'}, use_global_device_ids=true, to_apply=%region_6.9 | all-reduce | flops 256 | bytes 2048 | tf_op jit(solution)/shard_map/psum | solution.py:56
  190.1 0.1 copy.8
  190.2 1.5 cholesky.70
  191.6 0.6 compare_reduce_fusion.1
  192.3 0.6 fusion.30
  192.9 1.2 custom-call.8
  194.2 1.4 convolution_convert_fusion
  195.6 8.0 %fusion.57 = f32[16,2048]{1,0:T(8,128)S(1)} fusion(bf16[16,4096]{1,0:T(8,128)(2,1)S(1)} %convolution_convert_fusion, bf16[4096,2048]{1,0:T(8,128)(2,1)} %param.6), kind=kOutput, calls=%fused_computation.81 | convolution fusion | flops 268435456 | bytes 17039360 | tf_op jit(solution)/shard_map/dot_general | solution.py:68
  203.6 34.2 %all-reduce.12 = bf16[16,2048]{1,0:T(8,128)(2,1)S(1)} all-reduce(f32[16,2048]{1,0:T(8,128)S(1)} %fusion.57), channel_id=1, replica_groups=mesh['row'=8,'col'=4] {'row'}, use_global_device_ids=true, to_apply=%region_7.10 | all-reduce | flops 32768 | bytes 196608 | tf_op jit(solution)/shard_map/psum | solution.py:75
  237.8 10.9 %convolution_multiply_fusion = f32[16,4096]{1,0:T(8,128)} fusion(bf16[4096,2048]{1,0:T(8,128)(2,1)} %param.6, bf16[16,2048]{1,0:T(8,128)(2,1)S(1)} %all-reduce.12), kind=kOutput, calls=%fused_computation | convolution fusion | flops 268500992 | bytes 17104896 | tf_op jit(solution)/shard_map/dot_general | solution.py:48
  248.7 0.0 all-reduce.10.cloned.1.call-update
  248.8 30.4 %all-reduce.10.cloned.1.call-done = f32[16,4096]{1,0:T(8,128)} async-done(((f32[16,4096]{1,0:T(8,128)}), f32[16,4096]{1,0:T(8,128)}) %all-reduce.10.cloned.1.call-update) | async-done | bytes 262160 | tf_op jit(solution)/shard_map/psum | solution.py:55
  279.2 1.5 fusion.58
  280.6 21.6 %psum.63 = f32[16,16]{0,1:T(8,128)S(1)} all-reduce(f32[16,16]{0,1:T(8,128)S(1)} %fusion.58), channel_id=1, replica_groups=mesh['row'=8,'col'=4] {'row'}, use_global_device_ids=true, to_apply=%region_9.12 | all-reduce | flops 256 | bytes 2048 | tf_op jit(solution)/shard_map/psum | solution.py:56
  302.3 0.1 copy.10
  302.3 1.5 cholesky.81
  303.8 0.6 compare_reduce_fusion
  304.5 0.7 multiply_bitcast_fusion
  305.1 1.2 custom-call.9
  306.4 0.7 copy.11
  307.0 1.4 fusion.31
  308.4 0.6 dynamic-slice_multiply_fusion
  (6 shorter events, 0.1 us)
Async XLA Ops:
  7.2 47.5 %all-reduce.6.cloned.1.call-start = ((), (), s32[]{:S(2)}) async-start(), calls=%async_computation | async-start | bytes 524288 | tf_op jit(solution)/shard_map/psum | solution.py:55
  19.5 147.3 %all-reduce.8.cloned.1.call-start = ((), (), s32[]{:S(2)}) async-start(), calls=%async_computation.1 | async-start | bytes 524288 | tf_op jit(solution)/shard_map/psum | solution.py:55
  136.4 142.8 %all-reduce.10.cloned.1.call-start = ((), (), s32[]{:S(2)}) async-start(), calls=%async_computation.2 | async-start | bytes 524288 | tf_op jit(solution)/shard_map/psum | solution.py:55
Sparse Core Ops, SparseCore 0:
  19.6 34.9 all-reduce.5
  136.5 30.2 all-reduce.7
  248.9 30.2 all-reduce.9
where the time goes:
time: 316 us
  blocking collectives  133 us (42%)
  waiting for transfers between devices  95.9 us (30%)
  matrix products  58 us (18%)
  between operations  13.8 us (4%)
  other arithmetic  13.4 us (4%)
    psum x3, waiting for transfers between devices, body(): sketch = lax.psum(partial_sketch, 'col')  95.9 us
    psum x2, blocking collectives, body(): back = lax.psum(back_part, 'row')  68.4 us
    psum x3, blocking collectives, body(): lax.psum(jnp.dot(sketch, sketch.T, precision=lax.Precision.HIGHEST, prefe...  65 us
    dot_general x3, matrix products, project(): lax.dot_general(left, affinity, (((1,), (1,)), ((), ())), preferred_eleme...  33.4 us
    dot_general x2, matrix products, body(): jnp.dot(ortho.astype(jnp.bfloat16), affinity, preferred_element_type=jnp....  16.1 us
    another operation x9, other arithmetic, body(): lower = jnp.linalg.cholesky(gram)  6.39 us
  transfers between devices with their start and end apart: 3, of which 3 were waited for; matrix products, arithmetic and copies ran while one was open for 0% of the time, Pallas kernels for 0%

commit v1 on v0

--- a/solution.py
+++ b/solution.py
@@ -53,14 +53,18 @@
     partial_sketch = project(omega)
     for repeat in range(ITERS + 1):
         sketch = lax.psum(partial_sketch, "col")
-        gram = lax.psum(
+
+        def drive_digits(target):
+            z_new = lax.all_gather(target, "row").sum(axis=0)
+            return z_new
+
+        gram = drive_digits(
             jnp.dot(
                 sketch,
                 sketch.T,
                 precision=lax.Precision.HIGHEST,
                 preferred_element_type=jnp.float32,
-            ),
-            "row",
+            )
         )
         lower = jnp.linalg.cholesky(gram)
         ortho = lower_solve(lower, sketch)

time: 316 us -> 348 us (1.10)
  blocking collectives: 133 us -> 169 us
    all_gather x0 -> x3, blocking collectives: none -> 92 us  [drive_digits(): z_new = lax.all_gather(target, 'row').sum(axis=0)]
    psum x3 -> x0, blocking collectives: 65 us -> none  [body(): lax.psum(jnp.dot(sketch, sketch.T, precision=lax.Precision.HIGHEST, prefe...]
    psum x2, blocking collectives: 68.4 us -> 76.8 us  [body(): back = lax.psum(back_part, 'row')]
where the time goes in v1:
time: 348 us
  blocking collectives  169 us (49%)
  waiting for transfers between devices  92.6 us (27%)
  matrix products  58 us (17%)
  between operations  13.8 us (4%)
  other arithmetic  13.4 us (4%)
    psum x3, waiting for transfers between devices, body(): sketch = lax.psum(partial_sketch, 'col')  92.6 us
    all_gather x3, blocking collectives, drive_digits(): z_new = lax.all_gather(target, 'row').sum(axis=0)  92 us
    psum x2, blocking collectives, body(): back = lax.psum(back_part, 'row')  76.8 us
    dot_general x3, matrix products, project(): lax.dot_general(left, affinity, (((1,), (1,)), ((), ())), preferred_eleme...  33.4 us
    dot_general x2, matrix products, body(): jnp.dot(ortho.astype(jnp.bfloat16), affinity, preferred_element_type=jnp....  16.1 us
  transfers between devices with their start and end apart: 3, of which 3 were waited for; matrix products, arithmetic and copies ran while one was open for 0% of the time, Pallas kernels for 0%

profile of v1, /device:TPU:0, one launch (start us, length us, event | category | flops | bytes accessed | tf_op | source)
XLA Modules:
  0.0 347.7 jit_solution(17267427875380869731)
XLA Ops:
  7.2 0.0 all-reduce.6.cloned.1.call-start
  7.2 0.7 broadcast_multiply_fusion
  7.9 11.5 %fusion.12 = f32[16,4096]{1,0:T(8,128)} fusion(bf16[4096,2048]{1,0:T(8,128)(2,1)} %param.6, s32[2048]{0:T(1024)S(1)} %broadcast_multiply_fusion, s32[16]{0:T(128)} %param.7), kind=kOutput, calls=%fused_computation.22 | convolution fusion | flops 269418496 | bytes 17047616 | tf_op jit(solution)/shard_map/dot_general | solution.py:48
  19.5 0.0 all-reduce.6.cloned.1.call-update
  19.5 0.0 all-reduce.8.cloned.1.call-start
  19.5 35.1 %all-reduce.6.cloned.1.call-done = f32[16,4096]{1,0:T(8,128)} async-done(((f32[16,4096]{1,0:T(8,128)}), f32[16,4096]{1,0:T(8,128)}) %all-reduce.6.cloned.1.call-update) | async-done | bytes 262160 | tf_op jit(solution)/shard_map/psum | solution.py:55
  54.6 1.5 fusion.54
  56.1 30.6 %all-gather = f32[128,16]{1,0:T(8,128)S(1)} all-gather(f32[16,16]{1,0:T(8,128)S(1)} %fusion.54), channel_id=2, replica_groups=mesh['row'=8,'col'=4] {'row'}, dimensions={0}, use_global_device_ids=true | all-gather | bytes 9216 | tf_op jit(solution)/shard_map/all_gather | solution.py:58
  86.7 0.1 copy.9
  86.8 1.5 cholesky.59
  88.3 0.6 compare_reduce_fusion.2
  88.9 0.6 fusion.29
  89.6 1.2 custom-call.7
  90.8 1.4 convolution_convert_fusion.1
  92.2 8.0 %fusion.55 = f32[16,2048]{1,0:T(8,128)S(1)} fusion(bf16[16,4096]{1,0:T(8,128)(2,1)S(1)} %convolution_convert_fusion.1, bf16[4096,2048]{1,0:T(8,128)(2,1)} %param.6), kind=kOutput, calls=%fused_computation.79 | convolution fusion | flops 268435456 | bytes 17039360 | tf_op jit(solution)/shard_map/dot_general | solution.py:72
  100.3 38.4 %all-reduce.11 = bf16[16,2048]{1,0:T(8,128)(2,1)S(1)} all-reduce(f32[16,2048]{1,0:T(8,128)S(1)} %fusion.55), channel_id=1, replica_groups=mesh['row'=8,'col'=4] {'row'}, use_global_device_ids=true, to_apply=%region_4.7 | all-reduce | flops 32768 | bytes 196608 | tf_op jit(solution)/shard_map/psum | solution.py:79
  138.7 10.9 %convolution_multiply_fusion.1 = f32[16,4096]{1,0:T(8,128)} fusion(bf16[4096,2048]{1,0:T(8,128)(2,1)} %param.6, bf16[16,2048]{1,0:T(8,128)(2,1)S(1)} %all-reduce.11), kind=kOutput, calls=%fused_computation.1 | convolution fusion | flops 268500992 | bytes 17104896 | tf_op jit(solution)/shard_map/dot_general | solution.py:48
  149.6 0.0 all-reduce.8.cloned.1.call-update
  149.6 0.0 all-reduce.10.cloned.1.call-start
  149.7 28.7 %all-reduce.8.cloned.1.call-done = f32[16,4096]{1,0:T(8,128)} async-done(((f32[16,4096]{1,0:T(8,128)}), f32[16,4096]{1,0:T(8,128)}) %all-reduce.8.cloned.1.call-update) | async-done | bytes 262160 | tf_op jit(solution)/shard_map/psum | solution.py:55
  178.4 1.5 fusion.56
  179.8 30.8 %all-gather.1 = f32[128,16]{1,0:T(8,128)S(1)} all-gather(f32[16,16]{1,0:T(8,128)S(1)} %fusion.56), channel_id=3, replica_groups=mesh['row'=8,'col'=4] {'row'}, dimensions={0}, use_global_device_ids=true | all-gather | bytes 9216 | tf_op jit(solution)/shard_map/all_gather | solution.py:58
  210.7 0.1 copy.10
  210.7 1.5 cholesky.70
  212.2 0.6 compare_reduce_fusion.1
  212.9 0.6 fusion.30
  213.5 1.2 custom-call.8
  214.8 1.4 convolution_convert_fusion
  216.1 8.0 %fusion.57 = f32[16,2048]{1,0:T(8,128)S(1)} fusion(bf16[16,4096]{1,0:T(8,128)(2,1)S(1)} %convolution_convert_fusion, bf16[4096,2048]{1,0:T(8,128)(2,1)} %param.6), kind=kOutput, calls=%fused_computation.81 | convolution fusion | flops 268435456 | bytes 17039360 | tf_op jit(solution)/shard_map/dot_general | solution.py:72
  224.2 38.4 %all-reduce.12 = bf16[16,2048]{1,0:T(8,128)(2,1)S(1)} all-reduce(f32[16,2048]{1,0:T(8,128)S(1)} %fusion.57), channel_id=1, replica_groups=mesh['row'=8,'col'=4] {'row'}, use_global_device_ids=true, to_apply=%region_7.10 | all-reduce | flops 32768 | bytes 196608 | tf_op jit(solution)/shard_map/psum | solution.py:79
  262.6 10.9 %convolution_multiply_fusion = f32[16,4096]{1,0:T(8,128)} fusion(bf16[4096,2048]{1,0:T(8,128)(2,1)} %param.6, bf16[16,2048]{1,0:T(8,128)(2,1)S(1)} %all-reduce.12), kind=kOutput, calls=%fused_computation | convolution fusion | flops 268500992 | bytes 17104896 | tf_op jit(solution)/shard_map/dot_general | solution.py:48
  273.5 0.0 all-reduce.10.cloned.1.call-update
  273.5 28.7 %all-reduce.10.cloned.1.call-done = f32[16,4096]{1,0:T(8,128)} async-done(((f32[16,4096]{1,0:T(8,128)}), f32[16,4096]{1,0:T(8,128)}) %all-reduce.10.cloned.1.call-update) | async-done | bytes 262160 | tf_op jit(solution)/shard_map/psum | solution.py:55
  302.3 1.5 fusion.58
  303.8 30.6 %all-gather.2 = f32[128,16]{1,0:T(8,128)S(1)} all-gather(f32[16,16]{1,0:T(8,128)S(1)} %fusion.58), channel_id=4, replica_groups=mesh['row'=8,'col'=4] {'row'}, dimensions={0}, use_global_device_ids=true | all-gather | bytes 9216 | tf_op jit(solution)/shard_map/all_gather | solution.py:58
  334.4 0.1 copy.11
  334.5 1.5 cholesky.81
  336.0 0.6 compare_reduce_fusion
  336.6 0.7 multiply_bitcast_fusion
  337.3 1.2 custom-call.9
  338.5 0.7 copy.12
  339.2 1.4 fusion.31
  340.5 0.6 dynamic-slice_multiply_fusion
  (9 shorter events, 0.2 us)
Async XLA Ops:
  7.2 47.5 %all-reduce.6.cloned.1.call-start = ((), (), s32[]{:S(2)}) async-start(), calls=%async_computation | async-start | bytes 524288 | tf_op jit(solution)/shard_map/psum | solution.py:55
  19.5 158.9 %all-reduce.8.cloned.1.call-start = ((), (), s32[]{:S(2)}) async-start(), calls=%async_computation.1 | async-start | bytes 524288 | tf_op jit(solution)/shard_map/psum | solution.py:55
  149.6 152.7 %all-reduce.10.cloned.1.call-start = ((), (), s32[]{:S(2)}) async-start(), calls=%async_computation.2 | async-start | bytes 524288 | tf_op jit(solution)/shard_map/psum | solution.py:55
Sparse Core Ops, SparseCore 0:
  19.6 34.9 all-reduce.5
  149.7 28.5 all-reduce.7
  273.7 28.5 all-reduce.9
